TPU v7x, 512 devices: a whole 4x4x16 slice. The times are simulated.
512 devices in a mesh: rows: 16 (over z_lo, x), cols: 32 (over y, z_hi, core).
Axes of the slice: x: 4, y: 4, z: 16 (z_hi: 4, z_lo: 4; z = z_hi * 4 + z_lo), core: 2. Of those that a mesh axis runs over, the one named last changes fastest.
Arguments:
- file_pixels: bfloat16 [48, 512, 4096], P(None, ('rows', 'cols')), may hold values from -6 to 6
- patchify_weight: bfloat16 [64, 48], replicated, may hold values from -0.875 to 0.875
- patchify_bias: float32 [64], replicated, may hold values from -3 to 3
- norm_gain: float32 [64], replicated, may hold values from 0.5 to 1.5
- norm_offset_vector: float32 [64], replicated, may hold values from -3 to 3
- kernel: float32 [64, 49], replicated, may hold values from -0.875 to 0.875
- kernel_offset: float32 [64], replicated, may hold values from -3 to 3
- cotangent: bfloat16 [64, 512, 4096], P(None, 'rows', 'cols'), may hold values from -10 to 10, as said below
Outputs:
- stem_output: bfloat16 [64, 512, 4096], P(None, 'rows', 'cols')
- weight_grad: float32 [64, 48], replicated
- bias_grad: float32 [64], replicated
- norm_scale_gradient: float32 [64], replicated
- shift_grad: float32 [64], replicated
- kernel_grad: float32 [64, 49], replicated
- offset_grad: float32 [64], replicated
Inputs may be any that keep to these rules, and one draw needn't show every extreme that they name: A cotangent of order one.
All inputs are finite; a program needn't handle non-finite values.
Results may differ from a plain program's by a relative error of at most 0.0055.
Values may be sent and summed in bfloat16 or wider, within the bound.
A program may use at most 64 MiB of HBM per device.

v0:
```python
import math
import jax
import jax.numpy as jnp
from jax import lax
from jax.sharding import PartitionSpec as P

norm_eps = 1e-06
side = 7


def extended(block, sides, width):
    for axis, dim in sides:
        count = lax.axis_size(axis)
        forward = [(i, i + 1) for i in range(count - 1)]
        backward = [(target, source) for source, target in forward]
        low = lax.ppermute(
            lax.slice_in_dim(block, block.shape[dim] - width, None, axis=dim), axis, forward
        )
        high = lax.ppermute(lax.slice_in_dim(block, 0, width, axis=dim), axis, backward)
        block = jnp.concatenate([low, block, high], axis=dim)
    return block


def embed_patches(pixel_values, weight, bias):
    flat = pixel_values.reshape(pixel_values.shape[0], -1)
    mixed = jnp.dot(weight, flat, preferred_element_type=jnp.float32) + bias[:, None]
    return mixed.astype(jnp.bfloat16).reshape(
        weight.shape[0], pixel_values.shape[1], pixel_values.shape[2]
    )


def apply_layer_norm(patch_embedding):
    values = patch_embedding.astype(jnp.float32)
    center = values - jnp.mean(values, axis=0, keepdims=True)
    spread = jnp.mean(center * center, axis=0, keepdims=True)
    inverse_deviation = lax.rsqrt(spread + norm_eps)
    return (center * inverse_deviation, inverse_deviation)


def depthwise(padded, taps, height, breadth):
    total = jnp.zeros((padded.shape[0], height, breadth), jnp.float32)
    for tap_row in range(side):
        for tap_col in range(side):
            window = padded[:, tap_row : tap_row + height, tap_col : tap_col + breadth].astype(
                jnp.float32
            )
            total = total + taps[:, tap_row * side + tap_col][:, None, None] * window
    return total


def kernel_terms(padded, upstream, height, breadth):
    terms = []
    for tap_row in range(side):
        for tap_col in range(side):
            window = padded[:, tap_row : tap_row + height, tap_col : tap_col + breadth].astype(
                jnp.float32
            )
            terms.append(jnp.sum(window * upstream, axis=(1, 2)))
    return jnp.stack(terms, axis=1)


def per_device(
    file_pixels,
    patchify_weight,
    patchify_bias,
    norm_gain,
    norm_offset_vector,
    kernel,
    kernel_offset,
    cotangent,
):
    height = cotangent.shape[1]
    breadth = cotangent.shape[2]
    factor = 1.0 / math.sqrt(height * lax.axis_size("rows") * breadth * lax.axis_size("cols"))
    patch_embedding = lax.all_to_all(
        embed_patches(file_pixels, patchify_weight, patchify_bias),
        "cols",
        split_axis=2,
        concat_axis=1,
        tiled=True,
    )
    centered_input, inverse_deviation = apply_layer_norm(patch_embedding)
    scale_factor = norm_gain[:, None, None]
    normalized_output = (centered_input * scale_factor + norm_offset_vector[:, None, None]).astype(
        jnp.bfloat16
    )
    tall = extended(normalized_output, (("rows", 1),), 3)
    padded = extended(tall, (("cols", 2),), 3)
    cot_tall = extended(cotangent, (("rows", 1),), 3)
    cot_pad = extended(cot_tall, (("cols", 2),), 3)
    stem_output = (
        depthwise(padded, kernel, height, breadth) + kernel_offset[:, None, None]
    ).astype(jnp.bfloat16)
    upstream = cotangent.astype(jnp.float32) * factor
    kernel_grad = kernel_terms(padded, upstream, height, breadth)
    offset_grad = jnp.sum(upstream, axis=(1, 2))
    normalized_gradient = depthwise(cot_pad, kernel[:, ::-1], height, breadth) * factor
    norm_scale_gradient = jnp.sum(normalized_gradient * centered_input, axis=(1, 2))
    shift_grad = jnp.sum(normalized_gradient, axis=(1, 2))
    input_gradient = normalized_gradient * scale_factor
    patch_gradient = inverse_deviation * (
        input_gradient
        - jnp.mean(input_gradient, axis=0, keepdims=True)
        - centered_input * jnp.mean(input_gradient * centered_input, axis=0, keepdims=True)
    )
    patch_gradient = patch_gradient.astype(jnp.bfloat16)
    local_grad = lax.all_to_all(patch_gradient, "cols", split_axis=1, concat_axis=2, tiled=True)
    partial_weight = lax.dot_general(
        local_grad.reshape(local_grad.shape[0], -1),
        file_pixels.reshape(file_pixels.shape[0], -1),
        (((1,), (1,)), ((), ())),
        preferred_element_type=jnp.float32,
    )
    bias_part = jnp.sum(local_grad.astype(jnp.float32), axis=(1, 2))
    totals = lax.psum(
        (partial_weight, bias_part, norm_scale_gradient, shift_grad, kernel_grad, offset_grad),
        ("rows", "cols"),
    )
    return (stem_output, totals[0], totals[1], totals[2], totals[3], totals[4], totals[5])


def solution(mesh):
    return jax.shard_map(
        per_device,
        mesh=mesh,
        in_specs=(
            P(None, ("rows", "cols"), None),
            P(),
            P(),
            P(),
            P(),
            P(),
            P(),
            P(None, "rows", "cols"),
        ),
        out_specs=(P(None, "rows", "cols"), P(), P(), P(), P(), P(), P()),
        check_vma=False,
    )
```

profile of v0, /device:TPU:1, one launch (start us, length us, event | category | flops | bytes accessed | tf_op | source)
XLA Modules:
  0.0 420.4 jit_solution(11450217107587844098)
XLA Ops:
  6.0 22.4 %reduce.3 = bf16[4096,64]{1,0:T(8,128)(2,1)S(1)} reduce(bf16[4096,1,64]{2,1,0:T(2,128)(2,1)S(1)} %bitcast.174, bf16[]{:T(256)} %broadcast.111), dimensions={1}, to_apply=%bitcast.163.reduce_sub_computation | reduce | bytes 1048578
  29.9 19.6 %all-to-all-start = ((bf16[32,2,4096]{2,1,0:T(2,128)(2,1)}), bf16[32,2,4096]{2,1,0:T(2,128)(2,1)}, u32[]{:S(2)}, u32[]{:S(2)}) async-start(bf16[32,2,4096]{2,1,0:T(2,128)(2,1)} %reshape.173), calls=%async_computation | async-start | bytes 1048576 | tf_op jit(solution)/shard_map/all_to_all | solution.py:75
  51.4 3.1 collective-permute-start.4
  57.6 3.3 collective-permute-done.5
  61.0 8.4 %collective-permute-start.6 = (bf16[64,38,3]{0,1,2:T(8,128)(2,1)S(1)}, bf16[64,38,3]{0,1,2:T(8,128)(2,1)S(1)}, u32[]{:S(2)}, u32[]{:S(2)}) collective-permute-start(bf16[64,38,3]{0,1,2:T(8,128)(2,1)S(1)} %get-tuple-element.117), channel_id=1, source_target_pairs={{0,1},{1,2},{2,3},{3,4},{4,5},{5,6},{6,7},{7,8},{8,9},{9,10},{10,1... | collective-permute-start | bytes 43784 | tf_op jit(solution)/shard_map/ppermute | solution.py:16
  69.4 13.0 %collective-permute-start.7 = (bf16[64,38,3]{0,1,2:T(8,128)(2,1)S(1)}, bf16[64,38,3]{0,1,2:T(8,128)(2,1)S(1)}, u32[]{:S(2)}, u32[]{:S(2)}) collective-permute-start(bf16[64,38,3]{0,1,2:T(8,128)(2,1)S(1)} %get-tuple-element.118), channel_id=1, source_target_pairs={{1,0},{2,1},{3,2},{4,3},{5,4},{6,5},{7,6},{8,7},{9,8},{10,9},{11,1... | collective-permute-start | bytes 43784 | tf_op jit(solution)/shard_map/ppermute | solution.py:19
  83.0 3.8 maximum_maximum_fusion.1
  86.8 5.5 %reshape.174 = bf16[4096,1,64]{2,1,0:T(2,128)(2,1)} reshape(bf16[32,2,4096]{2,1,0:T(2,128)(2,1)} %all-to-all-done) | data formatting | bytes 1048576
  92.3 31.6 %convert_reduce_fusion.1 = f32[4096]{0:T(1024)S(1)} fusion(bf16[4096,1,64]{2,1,0:T(2,128)(2,1)} %reshape.174), kind=kLoop, calls=%fused_computation.334 | loop fusion | flops 520192 | bytes 540672 | tf_op jit(solution)/shard_map/reduce_sum | solution.py:34
  124.0 3.3 bitcast_convert_fusion
  127.2 58.9 %multiply_reduce_fusion.2 = f32[4096]{0:T(1024)S(1)} fusion(f32[4096]{0:T(1024)S(1)} %get-tuple-element.177, bf16[4096,1,64]{2,1,0:T(2,128)(2,1)S(1)} %copy-done.3), kind=kLoop, calls=%fused_computation.233 | loop fusion | flops 1044480 | bytes 557056 | tf_op jit(solution)/shard_map/reduce_sum | solution.py:35
  186.4 22.9 %multiply_reduce_fusion = (f32[64]{0:T(128)}, f32[32,128]{0,1:T(8,128)S(1)}, f32[32,128]{0,1:T(8,128)S(1)}, f32[64]{0:T(128)}, f32[64,32,128]{0,1,2:T(8,128)S(1)}) fusion(f32[32,128]{0,1:T(8,128)S(1)} %copy.97, f32[32,128]{0,1:T(8,128)S(1)} %copy.95, f32[64,32,128]{0,2,1:T(8,128)} %bitcast.172, f32[64]{0:T(128)} %broadcast_multiply_fusion.3, ...), kind=kLoop, calls=%fused_computation.228 | loop fusion | flops 45604736 | bytes 24818688 | tf_op jit(solution)/shard_map/reduce_sum | solution.py:98
  209.3 3.5 multiply_convert_fusion
  212.9 3.1 collective-permute-start
  218.0 3.8 collective-permute-done.1
  221.8 9.0 %collective-permute-start.2 = (bf16[64,38,3]{0,1,2:T(8,128)(2,1)S(1)}, bf16[64,38,3]{0,1,2:T(8,128)(2,1)S(1)}, u32[]{:S(2)}, u32[]{:S(2)}) collective-permute-start(bf16[64,38,3]{0,1,2:T(8,128)(2,1)S(1)} %get-tuple-element.121), channel_id=1, source_target_pairs={{0,1},{1,2},{2,3},{3,4},{4,5},{5,6},{6,7},{7,8},{8,9},{9,10},{10,1... | collective-permute-start | bytes 43784 | tf_op jit(solution)/shard_map/ppermute | solution.py:16
  234.6 14.7 %all-to-all-start.1 = ((bf16[64,32,128]{2,0,1:T(8,128)(2,1)}), bf16[64,32,128]{2,0,1:T(8,128)(2,1)S(1)}, u32[]{:S(2)}, u32[]{:S(2)}) async-start(bf16[64,32,128]{2,0,1:T(8,128)(2,1)} %copy.104), calls=%async_computation.1 | async-start | bytes 1048576 | tf_op jit(solution)/shard_map/all_to_all | solution.py:107
  249.4 4.1 maximum_maximum_fusion
  253.9 7.2 %fusion.148 = (f32[64]{0:T(128)}, f32[64]{0:T(128)}, f32[64]{0:T(128)}, f32[64]{0:T(128)}, f32[64]{0:T(128)}, /*index=5*/f32[64]{0:T(128)}, f32[64]{0:T(128)}, f...) fusion(bf16[64,32,128]{0,1,2:T(8,128)(2,1)S(1)} %copy-done.2, ...), kind=kLoop, calls=%fused_computation.200 | loop fusion | flops 14678912 | bytes 9966080 | tf_op jit(solution)/shard_map/reduce_sum | solution.py:58
  261.5 17.8 %add_convert_fusion = bf16[64,32,128]{0,1,2:T(8,128)(2,1)} fusion(bf16[64,32,128]{0,1,2:T(8,128)(2,1)S(1)} %copy-done.5, bf16[64,3,128]{0,1,2:T(4,128)(2,1)S(1)} %copy-done.8, bf16[64,3,128]{0,1,2:T(4,128)(2,1)S(1)} %collective-permute-done, f32[64]{0:T(128)} %param.14, f32[64]{0:T(128)S(1)} %copy-done.50, f32[64]{0:T(128)S(1)} %copy-done.51, ...), kind=kLoop, calls=%fused_computation.231 | loop fusion | flops 43515904 | bytes 23179776 | tf_op jit(solution)/shard_map/convert_element_type | solution.py:93
  279.3 4.6 %fusion.147 = (f32[64]{0:T(128)S(1)}, f32[64]{0:T(128)S(1)}, f32[64]{0:T(128)S(1)}, f32[64]{0:T(128)S(1)}, f32[64]{0:T(128)S(1)}, /*index=5*/f32[64]{0:T(128)S(1...) fusion(bf16[64,32,128]{0,1,2:T(8,128)(2,1)S(1)} %copy-done.2, ...), kind=kLoop, calls=%fused_computation.199 | loop fusion | flops 13106560 | bytes 2722304 | tf_op jit(solution)/shard_map/reduce_sum | solution.py:58
  283.9 3.6 copy.106
  288.5 6.8 %fusion.144 = (f32[64]{0:T(128)S(1)}, f32[64]{0:T(128)S(1)}, f32[64]{0:T(128)S(1)}, f32[64]{0:T(128)S(1)}, f32[64]{0:T(128)S(1)}, /*index=5*/f32[64]{0:T(128)S(1...) fusion(bf16[64,32,128]{0,1,2:T(8,128)(2,1)S(1)} %copy-done.2, ...), kind=kLoop, calls=%fused_computation.196 | loop fusion | flops 14940992 | bytes 9966336 | tf_op jit(solution)/shard_map/reduce_sum | solution.py:58
  296.1 123.9 %all-reduce = (f32[64,48]{0,1:T(8,128)}, f32[64]{0:T(128)}, f32[64]{0:T(128)}, f32[64]{0:T(128)}, f32[64,49]{0,1:T(8,128)}, /*index=5*/f32[64]{0:T(128)}) all-reduce(f32[64,48]{0,1:T(8,128)S(1)} %fusion.183, f32[64]{0:T(128)S(1)} %convert_reduce_fusion, f32[64]{0:T(128)S(1)} %copy-done.70, ...), channel_id=1, replica_groups=mesh['rows'=16,'cols'=32] {'rows','cols'}, use_global_device_ids=true, to_apply=%region_4.0 | all-reduce | flops 6464 | bytes 51712 | tf_op jit(solution)/shard_map/psum | solution.py:115
  (186 shorter events, 20.2 us)
Async XLA Ops:
  28.4 21.1 %copy-start.9 = (bf16[64,32,128]{2,1,0:T(8,128)(2,1)S(1)}, bf16[64,32,128]{2,1,0:T(8,128)(2,1)}, u32[]{:S(2)}) copy-start(bf16[64,32,128]{2,1,0:T(8,128)(2,1)} %param.15) | copy-start | bytes 1572868
  28.4 27.4 %copy-start.10 = (f32[64,49]{0,1:T(8,128)S(1)}, f32[64,49]{0,1:T(8,128)}, u32[]{:S(2)}) copy-start(f32[64,49]{0,1:T(8,128)} %param.13) | copy-start | bytes 37636
  29.9 52.5 %copy-start.73 = (f32[64]{0:T(128)S(1)}, f32[64]{0:T(128)}, u32[]{:S(2)}) copy-start(f32[64]{0:T(128)} %param.11) | copy-start | bytes 772
  29.9 56.8 %all-to-all-start = ((bf16[32,2,4096]{2,1,0:T(2,128)(2,1)}), bf16[32,2,4096]{2,1,0:T(2,128)(2,1)}, u32[]{:S(2)}, u32[]{:S(2)}) async-start(bf16[32,2,4096]{2,1,0:T(2,128)(2,1)} %reshape.173), calls=%async_computation | async-start | bytes 1048576 | tf_op jit(solution)/shard_map/all_to_all | solution.py:75
  51.2 31.7 %copy-start.1 = (bf16[64,32,128]{0,1,2:T(8,128)(2,1)}, bf16[64,32,128]{0,1,2:T(8,128)(2,1)S(1)}, u32[]{:S(2)}) copy-start(bf16[64,32,128]{0,1,2:T(8,128)(2,1)S(1)} %copy.98) | copy-start | bytes 1572868
  51.4 6.3 %collective-permute-start.4 = (bf16[64,3,128]{0,1,2:T(4,128)(2,1)S(1)}, bf16[64,3,128]{0,1,2:T(4,128)(2,1)S(1)}, u32[]{:S(2)}, u32[]{:S(2)}) collective-permute-start(bf16[64,3,128]{0,1,2:T(4,128)(2,1)S(1)} %get-tuple-element.123), channel_id=1, source_target_pairs={{0,32},{32,64},{64,96},{96,128},{128,160},{160,192},{192,224},{224... | collective-permute-start | bytes 147464 | tf_op jit(solution)/shard_map/ppermute | solution.py:16
  54.5 6.5 %collective-permute-start.5 = (bf16[64,3,128]{0,1,2:T(4,128)(2,1)S(1)}, bf16[64,3,128]{0,1,2:T(4,128)(2,1)S(1)}, u32[]{:S(2)}, u32[]{:S(2)}) collective-permute-start(bf16[64,3,128]{0,1,2:T(4,128)(2,1)S(1)} %get-tuple-element.124), channel_id=1, source_target_pairs={{32,0},{64,32},{96,64},{128,96},{160,128},{192,160},{224,192},{256... | collective-permute-start | bytes 147464 | tf_op jit(solution)/shard_map/ppermute | solution.py:19
  56.3 130.0 %copy-start.11 = (f32[64]{0:T(128)}, f32[64]{0:T(128)S(1)}, u32[]{:S(2)}) copy-start(f32[64]{0:T(128)S(1)} %get-tuple-element.139) | copy-start | bytes 772
  56.3 130.0 %copy-start.13 = (f32[64]{0:T(128)}, f32[64]{0:T(128)S(1)}, u32[]{:S(2)}) copy-start(f32[64]{0:T(128)S(1)} %get-tuple-element.140) | copy-start | bytes 772
  56.3 130.0 %copy-start.15 = (f32[64]{0:T(128)}, f32[64]{0:T(128)S(1)}, u32[]{:S(2)}) copy-start(f32[64]{0:T(128)S(1)} %get-tuple-element.141) | copy-start | bytes 772
  56.3 130.0 %copy-start.17 = (f32[64]{0:T(128)}, f32[64]{0:T(128)S(1)}, u32[]{:S(2)}) copy-start(f32[64]{0:T(128)S(1)} %get-tuple-element.142) | copy-start | bytes 772
  61.0 22.0 %collective-permute-start.6 = (bf16[64,38,3]{0,1,2:T(8,128)(2,1)S(1)}, bf16[64,38,3]{0,1,2:T(8,128)(2,1)S(1)}, u32[]{:S(2)}, u32[]{:S(2)}) collective-permute-start(bf16[64,38,3]{0,1,2:T(8,128)(2,1)S(1)} %get-tuple-element.117), channel_id=1, source_target_pairs={{0,1},{1,2},{2,3},{3,4},{4,5},{5,6},{6,7},{7,8},{8,9},{9,10},{10,1... | collective-permute-start | bytes 43784 | tf_op jit(solution)/shard_map/ppermute | solution.py:16
  69.4 13.5 %collective-permute-start.7 = (bf16[64,38,3]{0,1,2:T(8,128)(2,1)S(1)}, bf16[64,38,3]{0,1,2:T(8,128)(2,1)S(1)}, u32[]{:S(2)}, u32[]{:S(2)}) collective-permute-start(bf16[64,38,3]{0,1,2:T(8,128)(2,1)S(1)} %get-tuple-element.118), channel_id=1, source_target_pairs={{1,0},{2,1},{3,2},{4,3},{5,4},{6,5},{7,6},{8,7},{9,8},{10,9},{11,1... | collective-permute-start | bytes 43784 | tf_op jit(solution)/shard_map/ppermute | solution.py:19
  92.3 31.7 %copy-start.3 = (bf16[4096,1,64]{2,1,0:T(2,128)(2,1)S(1)}, bf16[4096,1,64]{2,1,0:T(2,128)(2,1)}, u32[]{:S(2)}) copy-start(bf16[4096,1,64]{2,1,0:T(2,128)(2,1)} %reshape.174) | copy-start | bytes 1572868
  186.4 22.9 %copy-start.6 = (f32[64,1,4096]{0,1,2:T(1,128)S(1)}, f32[64,1,4096]{0,1,2:T(1,128)}, u32[]{:S(2)}) copy-start(f32[64,1,4096]{0,1,2:T(1,128)} %bitcast_convert_fusion) | copy-start | bytes 3145732
  186.4 22.9 %copy-start.72 = (f32[64]{0:T(128)S(1)}, f32[64]{0:T(128)}, u32[]{:S(2)}) copy-start(f32[64]{0:T(128)} %broadcast_multiply_fusion.3) | copy-start | bytes 772
  186.4 22.9 %copy-start.74 = (f32[64]{0:T(128)S(1)}, f32[64]{0:T(128)}, u32[]{:S(2)}) copy-start(f32[64]{0:T(128)} %param.11) | copy-start | bytes 772
  186.4 22.9 %copy-start.75 = (f32[64]{0:T(128)S(1)}, f32[64]{0:T(128)}, u32[]{:S(2)}) copy-start(f32[64]{0:T(128)} %param.12) | copy-start | bytes 772
  212.9 5.1 %collective-permute-start = (bf16[64,3,128]{0,1,2:T(4,128)(2,1)S(1)}, bf16[64,3,128]{0,1,2:T(4,128)(2,1)S(1)}, u32[]{:S(2)}, u32[]{:S(2)}) collective-permute-start(bf16[64,3,128]{0,1,2:T(4,128)(2,1)S(1)} %get-tuple-element.125), channel_id=1, source_target_pairs={{0,32},{32,64},{64,96},{96,128},{128,160},{160,192},{192,224},{224... | collective-permute-start | bytes 147464 | tf_op jit(solution)/shard_map/ppermute | solution.py:16
  216.1 5.7 %collective-permute-start.1 = (bf16[64,3,128]{0,1,2:T(4,128)(2,1)S(1)}, bf16[64,3,128]{0,1,2:T(4,128)(2,1)S(1)}, u32[]{:S(2)}, u32[]{:S(2)}) collective-permute-start(bf16[64,3,128]{0,1,2:T(4,128)(2,1)S(1)} %get-tuple-element.126), channel_id=1, source_target_pairs={{32,0},{64,32},{96,64},{128,96},{160,128},{192,160},{224,192},{256... | collective-permute-start | bytes 147464 | tf_op jit(solution)/shard_map/ppermute | solution.py:19
  221.8 27.6 %copy-start.7 = (bf16[64,3,128]{0,1,2:T(4,128)(2,1)}, bf16[64,3,128]{0,1,2:T(4,128)(2,1)S(1)}, u32[]{:S(2)}) copy-start(bf16[64,3,128]{0,1,2:T(4,128)(2,1)S(1)} %collective-permute-done.1) | copy-start | bytes 147460
  221.8 27.5 %collective-permute-start.2 = (bf16[64,38,3]{0,1,2:T(8,128)(2,1)S(1)}, bf16[64,38,3]{0,1,2:T(8,128)(2,1)S(1)}, u32[]{:S(2)}, u32[]{:S(2)}) collective-permute-start(bf16[64,38,3]{0,1,2:T(8,128)(2,1)S(1)} %get-tuple-element.121), channel_id=1, source_target_pairs={{0,1},{1,2},{2,3},{3,4},{4,5},{5,6},{6,7},{7,8},{8,9},{9,10},{10,1... | collective-permute-start | bytes 43784 | tf_op jit(solution)/shard_map/ppermute | solution.py:16
  230.8 18.6 %collective-permute-start.3 = (bf16[64,38,3]{0,1,2:T(8,128)(2,1)S(1)}, bf16[64,38,3]{0,1,2:T(8,128)(2,1)S(1)}, u32[]{:S(2)}, u32[]{:S(2)}) collective-permute-start(bf16[64,38,3]{0,1,2:T(8,128)(2,1)S(1)} %get-tuple-element.122), channel_id=1, source_target_pairs={{1,0},{2,1},{3,2},{4,3},{5,4},{6,5},{7,6},{8,7},{9,8},{10,9},{11,1... | collective-permute-start | bytes 43784 | tf_op jit(solution)/shard_map/ppermute | solution.py:19
  234.6 61.0 %all-to-all-start.1 = ((bf16[64,32,128]{2,0,1:T(8,128)(2,1)}), bf16[64,32,128]{2,0,1:T(8,128)(2,1)S(1)}, u32[]{:S(2)}, u32[]{:S(2)}) async-start(bf16[64,32,128]{2,0,1:T(8,128)(2,1)} %copy.104), calls=%async_computation.1 | async-start | bytes 1048576 | tf_op jit(solution)/shard_map/all_to_all | solution.py:107
  (62 other events, 451.4 us)
where the time goes:
time: 428 us; the launch traced here: 420 us
  other arithmetic  188 us (44%)
  blocking collectives  124 us (29%)
  starting transfers between devices  75.4 us (18%)
  local copies, waits for them, and re-layouts  21.3 us (5%)
  waiting for transfers between devices  7.75 us (2%)
    psum x1, blocking collectives, per_device(): lax.psum((partial_weight, bias_part, norm_scale_gradient, shift_grad, ker...  124 us
    reduce_sum x1, other arithmetic, apply_layer_norm(): spread = jnp.mean(center * center, axis=0, keepdims=True)  58.9 us
    reduce_sum x1, other arithmetic, apply_layer_norm(): center = values - jnp.mean(values, axis=0, keepdims=True)  31.6 us
    ppermute x4, starting transfers between devices, extended(): lax.ppermute(lax.slice_in_dim(block, block.shape[dim] - width, None, axis...  23.7 us
    reduce_sum x1, other arithmetic, per_device(): jnp.sum(normalized_gradient * centered_input, axis=(1, 2))  22.9 us
    unnamed x1, other arithmetic  22.4 us
    all_to_all x1, starting transfers between devices, per_device(): lax.all_to_all(embed_patches(file_pixels, patchify_weight, patchify_bias)...  19.6 us
    reduce_sum x4, other arithmetic, kernel_terms(): terms.append(jnp.sum(window * upstream, axis=(1, 2)))  19.4 us
  transfers between devices with their start and end apart: 10, of which 3 were waited for; matrix products, arithmetic and copies ran while one was open for 13% of the time, Pallas kernels for 0%

commit v1 on v0

--- a/solution.py
+++ b/solution.py
@@ -72,13 +72,10 @@
     height = cotangent.shape[1]
     breadth = cotangent.shape[2]
     factor = 1.0 / math.sqrt(height * lax.axis_size("rows") * breadth * lax.axis_size("cols"))
-    patch_embedding = lax.all_to_all(
-        embed_patches(file_pixels, patchify_weight, patchify_bias),
-        "cols",
-        split_axis=2,
-        concat_axis=1,
-        tiled=True,
-    )
+    x = embed_patches(file_pixels, patchify_weight, patchify_bias)
+    shards = jnp.split(x, lax.axis_size("cols"), axis=2)
+    arrived = lax.all_to_all(jnp.stack(shards), "cols", 0, 0)
+    patch_embedding = jnp.concatenate(arrived, axis=1)
     centered_input, inverse_deviation = apply_layer_norm(patch_embedding)
     scale_factor = norm_gain[:, None, None]
     normalized_output = (centered_input * scale_factor + norm_offset_vector[:, None, None]).astype(

time: 428 us -> 275 us (0.64); the launches traced: 420 us -> 275 us
  other arithmetic: 188 us -> 39.5 us
  starting transfers between devices: 75.4 us -> 62.9 us
  local copies, waits for them, and re-layouts: 21.3 us -> 31.6 us
    reduce_sum x1, other arithmetic: 58.9 us -> 0.19 us  [apply_layer_norm(): spread = jnp.mean(center * center, axis=0, keepdims=True)]
    reduce_sum x1, other arithmetic: 31.6 us -> 0.11 us  [apply_layer_norm(): center = values - jnp.mean(values, axis=0, keepdims=True)]
    unnamed x1 -> x0, other arithmetic: 22.4 us -> none
    ppermute x4, starting transfers between devices: 17.5 us -> 7.78 us  [extended(): lax.ppermute(lax.slice_in_dim(block, 0, width, axis=dim), axis, backward)]
    reduce_sum x4, other arithmetic: 19.4 us -> 10.1 us  [kernel_terms(): terms.append(jnp.sum(window * upstream, axis=(1, 2)))]
    unnamed x157 -> x75, local copies, waits for them, and re-layouts: 14.2 us -> 22.1 us
    convert_element_type x1, other arithmetic: 17.8 us -> 10.4 us  [per_device(): stem_output = (depthwise(padded, kernel, height, breadth) + kernel_offset...]
    concatenate x2, other arithmetic: 7.89 us -> 0.96 us  [extended(): block = jnp.concatenate([low, block, high], axis=dim)]
  transfers between devices with their start and end apart: 10 -> 10, of which waited for: 3 -> 4; matrix products, arithmetic and copies ran while one was open for 13% -> 11% of each run, Pallas kernels for 0% -> 0%
where the time goes in v1:
time: 275 us
  blocking collectives  128 us (47%)
  starting transfers between devices  62.9 us (23%)
  other arithmetic  39.5 us (14%)
  local copies, waits for them, and re-layouts  31.6 us (11%)
  waiting for transfers between devices  9.87 us (4%)
    psum x1, blocking collectives, per_device(): lax.psum((partial_weight, bias_part, norm_scale_gradient, shift_grad, ker...  128 us
    ppermute x4, starting transfers between devices, extended(): lax.ppermute(lax.slice_in_dim(block, block.shape[dim] - width, None, axis...  22.7 us
    unnamed x75, local copies, waits for them, and re-layouts  22.1 us
    all_to_all x1, starting transfers between devices, per_device(): arrived = lax.all_to_all(jnp.stack(shards), 'cols', 0, 0)  19.4 us
    reduce_sum x1, other arithmetic, per_device(): jnp.sum(normalized_gradient * centered_input, axis=(1, 2))  16.2 us
    all_to_all x1, starting transfers between devices, per_device(): lax.all_to_all(patch_gradient, 'cols', split_axis=1, concat_axis=2, tiled...  13.1 us
    convert_element_type x1, other arithmetic, per_device(): stem_output = (depthwise(padded, kernel, height, breadth) + kernel_offset...  10.4 us
    reduce_sum x4, other arithmetic, kernel_terms(): terms.append(jnp.sum(window * upstream, axis=(1, 2)))  10.1 us
  transfers between devices with their start and end apart: 10, of which 4 were waited for; matrix products, arithmetic and copies ran while one was open for 11% of the time, Pallas kernels for 0%

profile of v1, /device:TPU:1, one launch (start us, length us, event | category | flops | bytes accessed | tf_op | source)
XLA Modules:
  0.0 274.5 jit_solution(17821440734200651115)
XLA Ops:
  22.2 19.4 %all-to-all-start = ((bf16[32,64,1,128]{3,1,2,0:T(8,128)(2,1)}), bf16[32,64,1,128]{3,1,2,0:T(8,128)(2,1)S(1)}, u32[]{:S(2)}, u32[]{:S(2)}) async-start(bf16[32,64,1,128]{3,1,2,0:T(8,128)(2,1)} %constant_dynamic-update-slice_fusion), calls=%async_computation | async-start | bytes 1048576 | tf_op jit(solution)/shard_map/all_to_all | solution.py:77
  41.7 3.1 %collective-permute-start.4 = (bf16[64,3,128]{2,0,1:T(8,128)(2,1)S(1)}, bf16[64,3,128]{2,0,1:T(8,128)(2,1)S(1)}, u32[]{:S(2)}, u32[]{:S(2)}) collective-permute-start(bf16[64,3,128]{2,0,1:T(8,128)(2,1)S(1)} %copy.105), channel_id=1, source_target_pairs={{0,32},{32,64},{64,96},{96,128},{128,160},{160,192},{192,224},{224... | collective-permute-start | bytes 147464 | tf_op jit(solution)/shard_map/ppermute | solution.py:16
  44.9 1.3 collective-permute-start.5
  46.8 3.1 %collective-permute-done.5 = bf16[64,3,128]{2,0,1:T(8,128)(2,1)S(1)} collective-permute-done((bf16[64,3,128]{2,0,1:T(8,128)(2,1)S(1)}, bf16[64,3,128]{2,0,1:T(8,128)(2,1)S(1)}, u32[]{:S(2)}, u32[]{:S(2)}) %collective-permute-start.5) | collective-permute-done | bytes 49184 | tf_op jit(solution)/shard_map/ppermute | solution.py:19
  50.0 1.3 fusion.240
  51.3 1.4 copy.37
  52.7 1.4 copy.40
  54.1 3.3 %collective-permute-start.7 = (bf16[64,38,3]{0,1,2:T(8,128)(2,1)S(1)}, bf16[64,38,3]{0,1,2:T(8,128)(2,1)S(1)}, u32[]{:S(2)}, u32[]{:S(2)}) collective-permute-start(bf16[64,38,3]{0,1,2:T(8,128)(2,1)S(1)} %copy.40), channel_id=1, source_target_pairs={{1,0},{2,1},{3,2},{4,3},{5,4},{6,5},{7,6},{8,7},{9,8},{10,9},{11,1... | collective-permute-start | bytes 43784 | tf_op jit(solution)/shard_map/ppermute | solution.py:19
  57.4 7.2 %collective-permute-start.6 = (bf16[64,38,3]{0,1,2:T(8,128)(2,1)S(1)}, bf16[64,38,3]{0,1,2:T(8,128)(2,1)S(1)}, u32[]{:S(2)}, u32[]{:S(2)}) collective-permute-start(bf16[64,38,3]{0,1,2:T(8,128)(2,1)S(1)} %copy.37), channel_id=1, source_target_pairs={{0,1},{1,2},{2,3},{3,4},{4,5},{5,6},{6,7},{7,8},{8,9},{9,10},{10,1... | collective-permute-start | bytes 43784 | tf_op jit(solution)/shard_map/ppermute | solution.py:16
  64.6 2.5 collective-permute-done.6
  67.1 1.1 copy.38
  71.4 16.2 %fusion.188 = (f32[64]{0:T(128)}, f32[32,128]{1,0:T(8,128)S(1)}, f32[32,128]{1,0:T(8,128)S(1)}, f32[64]{0:T(128)}, f32[64,32,128]{2,0,1:T(8,128)S(1)}) fusion(bf16[32,64,1,128]{3,1,2,0:T(8,128)(2,1)S(1)} %all-to-all-done, f32[32,128]{1,0:T(8,128)S(1)} %add_rsqrt_fusion, f32[32,128]{1,0:T(8,128)S(1)} %broadcast_multiply_fusion.2, ...), kind=kLoop, calls=%fused_computation.324 | loop fusion | flops 74178432 | bytes 5973504 | tf_op jit(solution)/shard_map/reduce_sum | solution.py:95
  87.6 1.3 fusion.187
  89.0 4.9 %collective-permute-start = (bf16[64,3,128]{2,0,1:T(8,128)(2,1)S(1)}, bf16[64,3,128]{2,0,1:T(8,128)(2,1)S(1)}, u32[]{:S(2)}, u32[]{:S(2)}) collective-permute-start(bf16[64,3,128]{2,0,1:T(8,128)(2,1)S(1)} %get-tuple-element.108), channel_id=1, source_target_pairs={{0,32},{32,64},{64,96},{96,128},{128,160},{160,192},{192,224},{224... | collective-permute-start | bytes 147464 | tf_op jit(solution)/shard_map/ppermute | solution.py:16
  93.9 1.3 collective-permute-start.1
  95.2 3.5 %collective-permute-done.1 = bf16[64,3,128]{2,0,1:T(8,128)(2,1)S(1)} collective-permute-done((bf16[64,3,128]{2,0,1:T(8,128)(2,1)S(1)}, bf16[64,3,128]{2,0,1:T(8,128)(2,1)S(1)}, u32[]{:S(2)}, u32[]{:S(2)}) %collective-permute-start.1) | collective-permute-done | bytes 49184 | tf_op jit(solution)/shard_map/ppermute | solution.py:19
  99.4 7.4 %collective-permute-start.2 = (bf16[64,38,3]{0,1,2:T(8,128)(2,1)S(1)}, bf16[64,38,3]{0,1,2:T(8,128)(2,1)S(1)}, u32[]{:S(2)}, u32[]{:S(2)}) collective-permute-start(bf16[64,38,3]{0,1,2:T(8,128)(2,1)S(1)} %copy.30), channel_id=1, source_target_pairs={{0,1},{1,2},{2,3},{3,4},{4,5},{5,6},{6,7},{7,8},{8,9},{9,10},{10,1... | collective-permute-start | bytes 43784 | tf_op jit(solution)/shard_map/ppermute | solution.py:16
  107.2 1.9 collective-permute-start.3
  109.1 13.1 %all-to-all-start.1 = ((bf16[64,32,128]{2,0,1:T(8,128)(2,1)}), bf16[64,32,128]{2,0,1:T(8,128)(2,1)S(1)}, u32[]{:S(2)}, u32[]{:S(2)}) async-start(bf16[64,32,128]{2,0,1:T(8,128)(2,1)} %get-tuple-element.101), calls=%async_computation.1 | async-start | bytes 1048576 | tf_op jit(solution)/shard_map/all_to_all | solution.py:104
  124.0 10.4 %add_convert_fusion = bf16[64,32,128]{2,0,1:T(8,128)(2,1)S(1)} fusion(bf16[64,32,128]{2,0,1:T(8,128)(2,1)S(1)} %get-tuple-element.102, bf16[64,3,128]{2,0,1:T(8,128)(2,1)S(1)} %collective-permute-done.1, bf16[64,3,128]{2,0,1:T(8,128)(2,1)S(1)} %collective-permute-done, f32[64]{0:T(128)S(1)} %copy-done.17, f32[64]{0:T(128)S(1)} %copy-done.12, ...), kind=kLoop, calls=%fused_computation.327 | loop fusion | flops 40370176 | bytes 23179776 | tf_op jit(solution)/shard_map/convert_element_type | solution.py:90
  136.3 1.9 fusion.145
  138.2 3.6 %fusion.144 = (f32[64]{0:T(128)S(1)}, f32[64]{0:T(128)S(1)}, f32[64]{0:T(128)S(1)}, f32[64]{0:T(128)S(1)}, f32[64]{0:T(128)S(1)}, /*index=5*/f32[64]{0:T(128)S(1...) fusion(bf16[64,38,131]{2,0,1:T(8,128)(2,1)S(1)} %get-tuple-elem, ...), kind=kLoop, calls=%fused_computation.280 | loop fusion | flops 14678912 | bytes 9966080 | tf_op jit(solution)/shard_map/reduce_sum | solution.py:58
  141.8 3.8 %fusion.148 = (f32[64]{0:T(128)S(1)}, f32[64]{0:T(128)S(1)}, f32[64]{0:T(128)S(1)}, f32[64]{0:T(128)S(1)}, f32[64]{0:T(128)S(1)}, /*index=5*/f32[64]{0:T(128)S(1...) fusion(bf16[64,38,131]{2,0,1:T(8,128)(2,1)S(1)} %get-tuple-elem, ...), kind=kLoop, calls=%fused_computation.284 | loop fusion | flops 14678912 | bytes 9966080 | tf_op jit(solution)/shard_map/reduce_sum | solution.py:58
  146.4 128.2 %all-reduce = (f32[64,48]{0,1:T(8,128)}, f32[64]{0:T(128)}, f32[64]{0:T(128)}, f32[64]{0:T(128)}, f32[64,49]{0,1:T(8,128)}, /*index=5*/f32[64]{0:T(128)}) all-reduce(f32[64,48]{0,1:T(8,128)S(1)} %fusion.234, f32[64]{0:T(128)S(1)} %convert_reduce_fusion, f32[64]{0:T(128)S(1)} %copy-done.15, ...), channel_id=1, replica_groups=mesh['rows'=16,'cols'=32] {'rows','cols'}, use_global_device_ids=true, to_apply=%region_4.0 | all-reduce | flops 6464 | bytes 51712 | tf_op jit(solution)/shard_map/psum | solution.py:112
  (109 shorter events, 30.6 us)
Async XLA Ops:
  0.6 1.0 copy-start
  2.7 39.0 %copy-start.1 = (bf16[64,32,128]{2,1,0:T(8,128)(2,1)S(1)}, bf16[64,32,128]{2,1,0:T(8,128)(2,1)}, u32[]{:S(2)}) copy-start(bf16[64,32,128]{2,1,0:T(8,128)(2,1)} %param.15) | copy-start | bytes 1572868
  4.5 41.7 %copy-start.4 = (f32[64,49]{0,1:T(8,128)S(1)}, f32[64,49]{0,1:T(8,128)}, u32[]{:S(2)}) copy-start(f32[64,49]{0,1:T(8,128)} %param.13) | copy-start | bytes 37636
  22.2 47.9 %all-to-all-start = ((bf16[32,64,1,128]{3,1,2,0:T(8,128)(2,1)}), bf16[32,64,1,128]{3,1,2,0:T(8,128)(2,1)S(1)}, u32[]{:S(2)}, u32[]{:S(2)}) async-start(bf16[32,64,1,128]{3,1,2,0:T(8,128)(2,1)} %constant_dynamic-update-slice_fusion), calls=%async_computation | async-start | bytes 1048576 | tf_op jit(solution)/shard_map/all_to_all | solution.py:77
  41.7 4.6 %collective-permute-start.4 = (bf16[64,3,128]{2,0,1:T(8,128)(2,1)S(1)}, bf16[64,3,128]{2,0,1:T(8,128)(2,1)S(1)}, u32[]{:S(2)}, u32[]{:S(2)}) collective-permute-start(bf16[64,3,128]{2,0,1:T(8,128)(2,1)S(1)} %copy.105), channel_id=1, source_target_pairs={{0,32},{32,64},{64,96},{96,128},{128,160},{160,192},{192,224},{224... | collective-permute-start | bytes 147464 | tf_op jit(solution)/shard_map/ppermute | solution.py:16
  44.9 5.1 %collective-permute-start.5 = (bf16[64,3,128]{2,0,1:T(8,128)(2,1)S(1)}, bf16[64,3,128]{2,0,1:T(8,128)(2,1)S(1)}, u32[]{:S(2)}, u32[]{:S(2)}) collective-permute-start(bf16[64,3,128]{2,0,1:T(8,128)(2,1)S(1)} %copy.106), channel_id=1, source_target_pairs={{32,0},{64,32},{96,64},{128,96},{160,128},{192,160},{224,192},{256... | collective-permute-start | bytes 147464 | tf_op jit(solution)/shard_map/ppermute | solution.py:19
  46.2 24.2 %copy-start.5 = (f32[64]{0:T(128)}, f32[64]{0:T(128)S(1)}, u32[]{:S(2)}) copy-start(f32[64]{0:T(128)S(1)} %get-tuple-element.158) | copy-start | bytes 772
  46.2 24.2 %copy-start.7 = (f32[64]{0:T(128)}, f32[64]{0:T(128)S(1)}, u32[]{:S(2)}) copy-start(f32[64]{0:T(128)S(1)} %get-tuple-element.159) | copy-start | bytes 772
  46.3 24.2 %copy-start.9 = (f32[64]{0:T(128)}, f32[64]{0:T(128)S(1)}, u32[]{:S(2)}) copy-start(f32[64]{0:T(128)S(1)} %get-tuple-element.160) | copy-start | bytes 772
  46.3 24.2 %copy-start.11 = (f32[64]{0:T(128)}, f32[64]{0:T(128)S(1)}, u32[]{:S(2)}) copy-start(f32[64]{0:T(128)S(1)} %get-tuple-element.161) | copy-start | bytes 772
  46.3 24.2 %copy-start.13 = (f32[64]{0:T(128)}, f32[64]{0:T(128)S(1)}, u32[]{:S(2)}) copy-start(f32[64]{0:T(128)S(1)} %get-tuple-element.162) | copy-start | bytes 772
  51.3 13.3 %copy-start.18 = (f32[64]{0:T(128)S(1)}, f32[64]{0:T(128)}, u32[]{:S(2)}) copy-start(f32[64]{0:T(128)} %param.11) | copy-start | bytes 772
  54.1 14.9 %collective-permute-start.7 = (bf16[64,38,3]{0,1,2:T(8,128)(2,1)S(1)}, bf16[64,38,3]{0,1,2:T(8,128)(2,1)S(1)}, u32[]{:S(2)}, u32[]{:S(2)}) collective-permute-start(bf16[64,38,3]{0,1,2:T(8,128)(2,1)S(1)} %copy.40), channel_id=1, source_target_pairs={{1,0},{2,1},{3,2},{4,3},{5,4},{6,5},{7,6},{8,7},{9,8},{10,9},{11,1... | collective-permute-start | bytes 43784 | tf_op jit(solution)/shard_map/ppermute | solution.py:19
  57.4 9.7 %collective-permute-start.6 = (bf16[64,38,3]{0,1,2:T(8,128)(2,1)S(1)}, bf16[64,38,3]{0,1,2:T(8,128)(2,1)S(1)}, u32[]{:S(2)}, u32[]{:S(2)}) collective-permute-start(bf16[64,38,3]{0,1,2:T(8,128)(2,1)S(1)} %copy.37), channel_id=1, source_target_pairs={{0,1},{1,2},{2,3},{3,4},{4,5},{5,6},{6,7},{7,8},{8,9},{9,10},{10,1... | collective-permute-start | bytes 43784 | tf_op jit(solution)/shard_map/ppermute | solution.py:16
  70.1 1.1 copy-start.2
  70.1 1.3 copy-start.3
  71.4 16.2 %copy-start.19 = (f32[64]{0:T(128)S(1)}, f32[64]{0:T(128)}, u32[]{:S(2)}) copy-start(f32[64]{0:T(128)} %param.12) | copy-start | bytes 772
  89.0 6.2 %collective-permute-start = (bf16[64,3,128]{2,0,1:T(8,128)(2,1)S(1)}, bf16[64,3,128]{2,0,1:T(8,128)(2,1)S(1)}, u32[]{:S(2)}, u32[]{:S(2)}) collective-permute-start(bf16[64,3,128]{2,0,1:T(8,128)(2,1)S(1)} %get-tuple-element.108), channel_id=1, source_target_pairs={{0,32},{32,64},{64,96},{96,128},{128,160},{160,192},{192,224},{224... | collective-permute-start | bytes 147464 | tf_op jit(solution)/shard_map/ppermute | solution.py:16
  93.9 4.8 %collective-permute-start.1 = (bf16[64,3,128]{2,0,1:T(8,128)(2,1)S(1)}, bf16[64,3,128]{2,0,1:T(8,128)(2,1)S(1)}, u32[]{:S(2)}, u32[]{:S(2)}) collective-permute-start(bf16[64,3,128]{2,0,1:T(8,128)(2,1)S(1)} %get-tuple-element.109), channel_id=1, source_target_pairs={{32,0},{64,32},{96,64},{128,96},{160,128},{192,160},{224,192},{256... | collective-permute-start | bytes 147464 | tf_op jit(solution)/shard_map/ppermute | solution.py:19
  99.4 22.8 %collective-permute-start.2 = (bf16[64,38,3]{0,1,2:T(8,128)(2,1)S(1)}, bf16[64,38,3]{0,1,2:T(8,128)(2,1)S(1)}, u32[]{:S(2)}, u32[]{:S(2)}) collective-permute-start(bf16[64,38,3]{0,1,2:T(8,128)(2,1)S(1)} %copy.30), channel_id=1, source_target_pairs={{0,1},{1,2},{2,3},{3,4},{4,5},{5,6},{6,7},{7,8},{8,9},{9,10},{10,1... | collective-permute-start | bytes 43784 | tf_op jit(solution)/shard_map/ppermute | solution.py:16
  107.2 15.4 %collective-permute-start.3 = (bf16[64,38,3]{0,1,2:T(8,128)(2,1)S(1)}, bf16[64,38,3]{0,1,2:T(8,128)(2,1)S(1)}, u32[]{:S(2)}, u32[]{:S(2)}) collective-permute-start(bf16[64,38,3]{0,1,2:T(8,128)(2,1)S(1)} %copy.32), channel_id=1, source_target_pairs={{1,0},{2,1},{3,2},{4,3},{5,4},{6,5},{7,6},{8,7},{9,8},{10,9},{11,1... | collective-permute-start | bytes 43784 | tf_op jit(solution)/shard_map/ppermute | solution.py:19
  109.1 36.8 %all-to-all-start.1 = ((bf16[64,32,128]{2,0,1:T(8,128)(2,1)}), bf16[64,32,128]{2,0,1:T(8,128)(2,1)S(1)}, u32[]{:S(2)}, u32[]{:S(2)}) async-start(bf16[64,32,128]{2,0,1:T(8,128)(2,1)} %get-tuple-element.101), calls=%async_computation.1 | async-start | bytes 1048576 | tf_op jit(solution)/shard_map/all_to_all | solution.py:104
  123.0 1.0 copy-start.6
  123.0 1.0 copy-start.8
  (6 other events, 5.1 us)
